TPU v7x, 32 devices: a whole 2x2x4 slice. The times are simulated.
32 devices in a mesh: psg: 8 (over z, x), mp: 4 (over y, core).
Axes of the slice: x: 2, y: 2, z: 4, core: 2. Of those that a mesh axis runs over, the one named last changes fastest.
Arguments:
- tokens: bfloat16 [8192, 4096], P('psg'), may hold values from -6 to 6
- lengths: int32 [32], P('psg'), may hold values from 32 to 256, as said below
- assignment: int32 [32], P('psg'), may hold values from 0 to 3, as said below
- retrieval: float32 [32], P('psg'), may hold values from -8 to 306
- enc_gain: float32 [4096], replicated, may hold values from 0.25 to 1.75
- enc_qkv: bfloat16 [3, 4096, 2048], P(None, 'psg', 'mp'), may hold values from -0.09375 to 0.09375
- position_bias: float32 [32, 32], P('mp'), may hold values from -6 to 306
- enc_output: bfloat16 [2048, 4096], P('mp', 'psg'), may hold values from -0.125 to 0.125
- final_gain: float32 [4096], replicated, may hold values from 0.25 to 1.75
- embedding: bfloat16 [32128, 4096], P('mp', 'psg'), may hold values from -18 to 18
- dec_tokens: int32 [4, 2], replicated, may hold values from 0 to 32127
- dec_gain: float32 [4096], P('psg'), may hold values from 0.25 to 1.75
- cross_query: bfloat16 [4096, 2048], P('psg', 'mp'), may hold values from -0.0234375 to 0.0234375
- cross_keyval: bfloat16 [2, 4096, 2048], P(None, 'psg', 'mp'), may hold values from -0.09375 to 0.09375
- cross_output: bfloat16 [2048, 4096], P('mp', 'psg'), may hold values from -0.25 to 0.25
Outputs:
- encoded: bfloat16 [8192, 4096], P('psg', 'mp')
- decoded: bfloat16 [4, 2, 4096], P(None, None, ('psg', 'mp'))
Inputs may be any that keep to these rules, and one draw needn't show every extreme that they name: Passage p holds real tokens in its first lengths[p] slots and padding after them; in every draw all passages of some index of psg have 256 real tokens. `assignment`: every claim has exactly 8 passages.
All inputs are finite; a program needn't handle non-finite values.
Results may differ from a plain program's by a relative error of at most 0.013.
The roundings to bfloat16 on the way count: a program that leaves them out, or rounds other values in their place, can miss the bound.
Values may be sent and summed in bfloat16 or wider, within the bound.
No kernel may reach another device: no remote copies, remote signals or barrier semaphores. Data moves between devices by JAX's collectives and lax.ppermute only.
A program may use at most 128 MiB of HBM per device.

v0:
```python
import math
import jax
import jax.numpy as jnp
import numpy as np
from jax import lax
from jax.sharding import PartitionSpec as P

D = 4096
HEAD_DIM = 64
BUCKETS = 32
MAXDIST = 128
SEQ = 256
CLAIMS = 4
POS = 2
EPSILON = 1e-06
MASKED = -1e30
HIGHEST = lax.Precision.HIGHEST


def merged(value, axis, combine):
    everything = jax.tree.map(lambda part: lax.all_gather(part, axis), value)
    first = jax.tree.map(lambda part: part[0], everything)

    def turn(k, so_far):
        return combine(so_far, jax.tree.map(lambda part: part[k], everything))

    return lax.fori_loop(1, lax.axis_size(axis), turn, first)


def bucket_onehot(length, buckets, max_distance):
    halfway = buckets // 2
    exact_max = halfway // 2
    relative_list = list(range(-(length - 1), length))
    beyond_list = [
        min(
            halfway - 1,
            exact_max
            + math.floor(
                math.log(max(abs(shift), 1) / exact_max)
                / math.log(max_distance / exact_max)
                * (halfway - exact_max)
            ),
        )
        for shift in relative_list
    ]
    relative = np.array(relative_list)
    beyond = np.array(beyond_list)
    distance = np.abs(relative)
    bucket_ids = np.where(relative > 0, halfway, 0) + np.where(
        distance < exact_max, distance, beyond
    )
    return (bucket_ids[None, :] == np.arange(buckets)[:, None]).astype(np.float32)


def toeplitz(vectors):
    heads_count, width_all = vectors.shape
    length = (width_all + 1) // 2
    padded = jnp.concatenate([vectors, jnp.zeros((heads_count, 1), vectors.dtype)], axis=1)
    rolled = jnp.roll(padded, -(length - 1), axis=1)
    repeated = jnp.tile(rolled, (1, length))[:, : length * (2 * length - 1)]
    return repeated.reshape(heads_count, length, 2 * length - 1)[:, :, :length]


def rms_norm(values, norm_gain):
    values = values.astype(jnp.float32)
    inverse = lax.rsqrt(jnp.mean(values * values, axis=-1, keepdims=True) + EPSILON)
    return values * inverse * norm_gain


def combine_partial(first, second):
    first_max, first_total, first_acc = first
    second_max, second_total, second_acc = second
    joint_max = jnp.maximum(first_max, second_max)
    first_scale = jnp.exp(first_max - joint_max)
    second_scale = jnp.exp(second_max - joint_max)
    joint_total = first_total * first_scale + second_total * second_scale
    joint_acc = first_acc * first_scale[..., None] + second_acc * second_scale[..., None]
    return (joint_max, joint_total, joint_acc)


def shards(
    tokens,
    lengths,
    assignment,
    retrieval,
    enc_gain,
    enc_qkv,
    position_bias,
    enc_output,
    final_gain,
    embedding,
    dec_tokens,
    dec_gain,
    cross_query,
    cross_keyval,
    cross_output,
):
    tok_rows = tokens.shape[0]
    model_width = tokens.shape[1]
    passages_here = lengths.shape[0]
    width_here = enc_qkv.shape[1]
    inner_here = enc_qkv.shape[2]
    heads_here = inner_here // HEAD_DIM
    query_rows = CLAIMS * POS
    positions = jnp.arange(SEQ)
    groups_count = lax.axis_size("mp")
    normed = rms_norm(tokens, enc_gain).astype(jnp.bfloat16)
    projected = jnp.einsum(
        "td,kdc->ktc",
        normed,
        lax.all_gather(enc_qkv, "psg", axis=1, tiled=True),
        preferred_element_type=jnp.float32,
    )
    shaped = projected.astype(jnp.bfloat16).reshape(3, passages_here, SEQ, heads_here, HEAD_DIM)
    bias_table = jnp.dot(
        position_bias, jnp.asarray(bucket_onehot(SEQ, BUCKETS, MAXDIST)), precision=HIGHEST
    )
    pair_bias = toeplitz(bias_table)
    scores = (
        jnp.einsum("pihd,pjhd->phij", shaped[0], shaped[1], preferred_element_type=jnp.float32)
        + pair_bias[None]
    )
    valid_keys = positions[None, :] < lengths[:, None]
    scores = jnp.where(valid_keys[:, None, None, :], scores, MASKED)
    weights = jnp.exp(scores - jnp.max(scores, axis=-1, keepdims=True))
    probabilities = (weights / jnp.sum(weights, axis=-1, keepdims=True)).astype(jnp.bfloat16)
    attended = jnp.einsum(
        "phij,pjhd->pihd", probabilities, shaped[2], preferred_element_type=jnp.float32
    )
    attended = attended.astype(jnp.bfloat16).reshape(tok_rows, inner_here)
    share_width = model_width // groups_count
    share_start = lax.axis_index("mp") * share_width
    partial_out = jnp.dot(
        attended,
        lax.all_gather(enc_output, "psg", axis=1, tiled=True),
        preferred_element_type=jnp.float32,
    ).astype(jnp.bfloat16)
    summed = lax.psum(partial_out, "mp").astype(jnp.float32)
    encoded_full = (tokens.astype(jnp.float32) + summed).astype(jnp.bfloat16)
    encoded = lax.dynamic_slice_in_dim(encoded_full, share_start, share_width, 1)
    memory = rms_norm(encoded_full, final_gain).astype(jnp.bfloat16)
    vocab_here = embedding.shape[0]
    token_ids = dec_tokens.reshape(-1) - lax.axis_index("mp") * vocab_here
    lookup = (token_ids[:, None] == jnp.arange(vocab_here)[None, :]).astype(jnp.bfloat16)
    found_rows = jnp.dot(lookup, embedding, preferred_element_type=jnp.float32).astype(jnp.bfloat16)
    embedded = lax.psum(found_rows, "mp").astype(jnp.float32)
    query_weight = cross_query.astype(jnp.float32)
    squares_dec = lax.psum(jnp.sum(embedded * embedded, axis=1), "psg")
    dquery = embedded * lax.rsqrt(squares_dec / D + EPSILON)[:, None] * dec_gain
    cquery = lax.psum(jnp.dot(dquery, query_weight, precision=HIGHEST), "psg")
    cquery = cquery.reshape(query_rows, heads_here, HEAD_DIM)
    row_claim = jnp.arange(query_rows) // POS
    usable = (row_claim[:, None, None] == assignment[None, :, None]) & (
        positions[None, None, :] < lengths[None, :, None]
    )
    usable = usable.reshape(query_rows, 1, tok_rows)
    key_bias = jnp.broadcast_to(retrieval[:, None], (passages_here, SEQ)).reshape(tok_rows)
    key_weight = cross_keyval[0].astype(jnp.float32).reshape(width_here, heads_here, HEAD_DIM)
    folded = jnp.einsum("rhj,dhj->rhd", cquery, key_weight, precision=HIGHEST)
    folded_all = lax.all_gather(folded.astype(jnp.bfloat16), "psg", axis=2, tiled=True).astype(
        folded.dtype
    )
    memory_wide = memory.astype(jnp.float32)
    cross_scores = jnp.einsum("td,rhd->rht", memory_wide, folded_all, precision=HIGHEST) + key_bias
    masked = jnp.where(usable, cross_scores, MASKED)
    local_max = jnp.max(masked, axis=-1)
    weights_c = jnp.where(usable, jnp.exp(masked - local_max[..., None]), 0.0)
    local_max, weights_c = (local_max, weights_c)
    local_total = jnp.sum(weights_c, axis=-1)
    pooled = jnp.einsum("rht,td->rhd", weights_c, memory_wide, precision=HIGHEST)
    joint_max, joint_total, joint_pool = merged(
        (local_max, local_total, pooled), "psg", combine_partial
    )
    own_pool = (
        lax.dynamic_slice_in_dim(joint_pool, lax.axis_index("psg") * width_here, width_here, 2)
        / joint_total[..., None]
    )
    value_weight = cross_keyval[1].astype(jnp.float32).reshape(width_here, heads_here, HEAD_DIM)
    value_terms = jnp.einsum("rhd,dhj->rhj", own_pool, value_weight, precision=HIGHEST)
    cross_attn = lax.psum(value_terms, "psg")
    out_part = jnp.dot(
        cross_attn.reshape(query_rows, inner_here),
        cross_output.astype(jnp.float32),
        precision=HIGHEST,
    )
    out_share = lax.psum_scatter(out_part, "mp", scatter_dimension=1, tiled=True)
    piece_width = out_share.shape[1]
    residual = lax.dynamic_slice_in_dim(
        embedded, lax.axis_index("mp") * piece_width, piece_width, 1
    )
    decoded = (residual + out_share).astype(jnp.bfloat16).reshape(CLAIMS, POS, piece_width)
    return (encoded, decoded)


def solution(mesh):
    in_specs = (
        P("psg", None),
        P("psg"),
        P("psg"),
        P("psg"),
        P(),
        P(None, "psg", "mp"),
        P("mp", None),
        P("mp", "psg"),
        P(),
        P("mp", "psg"),
        P(),
        P("psg"),
        P("psg", "mp"),
        P(None, "psg", "mp"),
        P("mp", "psg"),
    )
    out_specs = (P("psg", "mp"), P(None, None, ("psg", "mp")))
    return jax.shard_map(shards, mesh=mesh, in_specs=in_specs, out_specs=out_specs, check_vma=False)
```

profile of v0, /device:TPU:0, one launch (start us, length us, event | category | flops | bytes accessed | tf_op | source)
XLA Modules:
  0.0 641.4 jit_solution(5036497669544402802)
XLA Ops:
  10.4 2.2 slice.61
  12.6 7.9 %reshape.172 = f32[8,256,511]{2,1,0:T(8,128)} reshape(f32[8,130816]{1,0:T(8,128)} %slice.61) | data formatting | bytes 8372224 | tf_op jit(solution)/shard_map/reshape | solution.py:61
  20.5 2.2 slice.62
  22.7 2.1 copy.44
  24.9 5.1 fusion.7
  29.9 159.1 %all-gather.7.cloned.1.call-done = bf16[3,4096,512]{2,1,0:T(8,128)(2,1)} async-done(((bf16[3,512,512]{2,1,0:T(8,128)(2,1)}), bf16[3,4096,512]{2,1,0:T(8,128)(2,1)}) %all-gather.7.cloned.1.call-update) | async-done | bytes 12582928 | tf_op jit(solution)/shard_map/all_gather | solution.py:111
  189.0 18.3 %convert_bitcast_fusion = bf16[3,1024,512]{2,1,0:T(8,128)(2,1)S(1)} fusion(bf16[3,4096,512]{2,1,0:T(8,128)(2,1)} %all-gather.7.cloned.1.call-done, bf16[1024,4096]{1,0:T(8,128)(2,1)} %param.18, f32[4096]{0:T(1024)S(1)} %copy-done.10, f32[1024]{0:T(1024)S(1)} %add_rsqrt_fusion.1), kind=kOutput, calls=%fused_computation.37 | convolution fusion | flops 12903251968 | bytes 24137728 | tf_op jit(solution)/shard_map/td,kdc->ktc/dot_general | solution.py:108
  209.1 2.8 reshape.191
  211.9 3.9 reshape.192
  215.8 3.9 reshape.190
  219.6 3.0 fusion.28
  222.7 5.4 fusion.64
  228.0 4.5 fusion.35
  233.5 30.4 %all-gather.9.cloned.1.call-done = bf16[512,4096]{1,0:T(8,128)(2,1)} async-done(((bf16[512,512]{1,0:T(8,128)(2,1)}), bf16[512,4096]{1,0:T(8,128)(2,1)}) %all-gather.9.cloned.1.call-update) | async-done | bytes 4194320 | tf_op jit(solution)/shard_map/all_gather | solution.py:135
  263.9 8.9 %convolution_convert_fusion = bf16[1024,4096]{1,0:T(8,128)(2,1)} fusion(bf16[1024,512]{0,1:T(8,128)(2,1)S(1)} %bitcast.81, bf16[512,4096]{1,0:T(8,128)(2,1)} %all-gather.9.cloned.1.call-done), kind=kOutput, calls=%fused_computation.29 | convolution fusion | flops 4299161600 | bytes 13631488 | tf_op jit(solution)/shard_map/dot_general | solution.py:133
  273.7 5.1 convolution_convert_fusion.2
  278.8 6.7 %psum.36 = bf16[8,512]{1,0:T(8,128)(2,1)S(1)} all-reduce(bf16[8,512]{1,0:T(8,128)(2,1)S(1)} %convolution_convert_fusion.2), channel_id=1, replica_groups=mesh['psg'=8,'mp'=4] {'mp'}, use_global_device_ids=true, to_apply=%region_4.5 | all-reduce | flops 4096 | bytes 16384 | tf_op jit(solution)/shard_map/psum | solution.py:146
  285.7 19.2 %psum.37 = f32[8]{0:T(128)S(1)} all-reduce(f32[8]{0:T(128)S(1)} %multiply_reduce_fusion), channel_id=1, replica_groups=mesh['psg'=8,'mp'=4] {'psg'}, use_global_device_ids=true, to_apply=%region_6.7 | all-reduce | flops 8 | bytes 64 | tf_op jit(solution)/shard_map/psum | solution.py:148
  305.8 33.1 %psum.38 = f32[8,8,64]{2,0,1:T(8,128)S(1)} all-reduce(f32[8,8,64]{2,0,1:T(8,128)S(1)} %copy.49), channel_id=1, replica_groups=mesh['psg'=8,'mp'=4] {'psg'}, use_global_device_ids=true, to_apply=%region_7.8 | all-reduce | flops 4096 | bytes 32768 | tf_op jit(solution)/shard_map/psum | solution.py:150
  339.4 31.5 %all_gather.29 = bf16[8,8,4096]{2,0,1:T(8,128)(2,1)S(1)} all-gather(bf16[8,8,512]{2,0,1:T(8,128)(2,1)S(1)} %fusion.44), channel_id=1, replica_groups=mesh['psg'=8,'mp'=4] {'psg'}, dimensions={2}, use_global_device_ids=true | all-gather | bytes 589824 | tf_op jit(solution)/shard_map/all_gather | solution.py:160
  370.9 53.5 %all-reduce.3.cloned.1.call-done = bf16[1024,4096]{1,0:T(8,128)(2,1)} async-done(((bf16[1024,4096]{1,0:T(8,128)(2,1)}), bf16[1024,4096]{1,0:T(8,128)(2,1)}) %all-reduce.3.cloned.1.call-update) | async-done | bytes 8388624 | tf_op jit(solution)/shard_map/psum | solution.py:138
  424.4 7.8 %fusion.4 = (f32[1024]{0:T(1024)S(1)}, bf16[1024,4096]{1,0:T(8,128)(2,1)S(1)}) fusion(bf16[1024,4096]{1,0:T(8,128)(2,1)} %all-reduce.3.cloned.1.call-done, bf16[1024,4096]{1,0:T(8,128)(2,1)} %param.18), kind=kLoop, calls=%fused_computation.14 | loop fusion | flops 29359104 | bytes 25169920 | tf_op jit(solution)/shard_map/reduce_sum | solution.py:66
  432.2 2.9 fusion.65
  435.4 6.4 %fusion.18 = f32[8,8,4096]{2,1,0:T(8,128)} fusion(bf16[1024,4096]{1,0:T(8,128)(2,1)S(1)} %get-tuple-element.200, f32[4096]{0:T(1024)S(1)} %copy-done.11, f32[1024]{0:T(1024)S(1)} %add_rsqrt_fusion, f32[8,8,1024]{2,1,0:T(8,128)S(1)} %get-tuple-element.209, f32[8,8]{1,0:T(8,128)S(1)} %get-tuple-element.208, pred[8,1024]{1,0:T(8,128)(4,1)S(1)} %broadcast_and_fusion), kind=kOutput, calls=%fused_computation.31 | convolution fusion | flops 3238133760 | bytes 9728256 | tf_op jit(solution)/shard_map/rht,td->rhd/dot_general | solution.py:170
  442.3 31.6 %all-gather.1 = f32[64,8]{1,0:T(8,128)S(1)} all-gather(f32[8,8]{1,0:T(8,128)S(1)} %fusion.46), channel_id=3, replica_groups=mesh['psg'=8,'mp'=4] {'psg'}, dimensions={0}, use_global_device_ids=true | all-gather | bytes 2304 | tf_op jit(solution)/shard_map/all_gather | solution.py:21
  474.0 31.6 %all-gather = f32[64,8]{1,0:T(8,128)S(1)} all-gather(f32[8,8]{1,0:T(8,128)S(1)} %get-tuple-element.208), channel_id=2, replica_groups=mesh['psg'=8,'mp'=4] {'psg'}, dimensions={0}, use_global_device_ids=true | all-gather | bytes 2304 | tf_op jit(solution)/shard_map/all_gather | solution.py:21
  505.6 61.5 %all-gather.11.cloned.1.call-done = f32[64,8,4096]{2,1,0:T(8,128)} async-done(((f32[8,8,4096]{2,1,0:T(8,128)}), f32[64,8,4096]{2,1,0:T(8,128)}) %all-gather.11.cloned.1.call-update) | async-done | bytes 8388624 | tf_op jit(solution)/shard_map/all_gather | solution.py:21
  568.4 12.4 %while.19 = (s32[]{:T(128)}, f32[8,8]{1,0:T(8,128)S(1)}, f32[8,8]{1,0:T(8,128)S(1)}, f32[8,8,4096]{2,1,0:T(8,128)S(1)}, f32[8,8,8]{2,1,0:T(8,128)S(1)}, /*index=...) while((s32[]{:T(128)}, f32[8,8]{1,0:T(8,128)S(1)}, ...), condition=%wide.region_12.13_spmd, body=%wide.region_11.12_spmd.sunk | while | flops 786821 | bytes 3148439 | solution.py:27
  568.4 1.8 fusion.82
  581.5 34.2 %psum.39 = f32[8,512]{1,0:T(8,128)S(1)} all-reduce(f32[8,512]{1,0:T(8,128)S(1)} %reshape.177), channel_id=1, replica_groups=mesh['psg'=8,'mp'=4] {'psg'}, use_global_device_ids=true, to_apply=%region_13.14 | all-reduce | flops 4096 | bytes 32768 | tf_op jit(solution)/shard_map/psum | solution.py:180
  616.7 3.1 constant_dynamic-slice_fusion
  619.8 13.8 %reduce-scatter.2.cloned.1.call-done = f32[8,128]{1,0:T(8,128)} async-done(((f32[8,512]{1,0:T(8,128)}), f32[8,128]{1,0:T(8,128)}) %reduce-scatter.2.cloned.1.call-update) | async-done | bytes 4112 | tf_op jit(solution)/shard_map/reduce_scatter | solution.py:186
  (93 shorter events, 23.7 us)
Async XLA Ops:
  7.2 297.7 %copy-start = (bf16[512,512]{1,0:T(8,128)(2,1)S(1)}, bf16[512,512]{1,0:T(8,128)(2,1)}, u32[]{:S(2)}) copy-start(bf16[512,512]{1,0:T(8,128)(2,1)} %param.30) | copy-start | bytes 1572868
  7.2 181.8 %all-gather.7.cloned.1.call-start = ((), (), s32[]{:S(2)}) async-start(), calls=%async_computation.1 | async-start | bytes 14155776 | tf_op jit(solution)/shard_map/all_gather | solution.py:111
  7.9 256.0 %all-gather.9.cloned.1.call-start = ((), (), s32[]{:S(2)}) async-start(), calls=%async_computation.2 | async-start | bytes 4718592 | tf_op jit(solution)/shard_map/all_gather | solution.py:135
  8.7 415.7 %all-reduce.3.cloned.1.call-start = ((), (), s32[]{:S(2)}) async-start(), calls=%async_computation.3 | async-start | bytes 16777216 | tf_op jit(solution)/shard_map/psum | solution.py:138
  12.6 12.1 %copy-start.9 = (s32[4]{0:T(128)S(1)}, s32[4]{0:T(128)}, u32[]{:S(2)}) copy-start(s32[4]{0:T(128)} %param.19) | copy-start | bytes 52
  20.5 168.5 %copy-start.10 = (f32[4096]{0:T(1024)S(1)}, f32[4096]{0:T(1024)}, u32[]{:S(2)}) copy-start(f32[4096]{0:T(1024)} %param.22) | copy-start | bytes 49156
  219.6 3.0 copy-start.3
  222.7 5.4 copy-start.2
  272.8 0.7 copy-start.7
  272.9 32.0 %copy-start.6 = (f32[512]{0:T(512)S(1)}, f32[512]{0:T(512)}, u32[]{:S(2)}) copy-start(f32[512]{0:T(512)} %param.29) | copy-start | bytes 6148
  272.9 32.4 %copy-start.4 = (bf16[2,512,512]{2,1,0:T(8,128)(2,1)S(1)}, bf16[2,512,512]{2,1,0:T(8,128)(2,1)}, u32[]{:S(2)}) copy-start(bf16[2,512,512]{2,1,0:T(8,128)(2,1)} %param.31) | copy-start | bytes 3145732
  272.9 294.2 %all-gather.11.cloned.1.call-start = ((), (), s32[]{:S(2)}) async-start(), calls=%async_computation.5 | async-start | bytes 9437184 | tf_op jit(solution)/shard_map/all_gather | solution.py:21
  273.7 31.9 %copy-start.8 = (f32[4]{0:T(128)S(1)}, f32[4]{0:T(128)}, u32[]{:S(2)}) copy-start(f32[4]{0:T(128)} %param.21) | copy-start | bytes 52
  273.7 65.2 %copy-start.12 = (s32[4]{0:T(128)S(1)}, s32[4]{0:T(128)}, u32[]{:S(2)}) copy-start(s32[4]{0:T(128)} %param.20) | copy-start | bytes 52
  370.9 61.3 %copy-start.11 = (f32[4096]{0:T(1024)S(1)}, f32[4096]{0:T(1024)}, u32[]{:S(2)}) copy-start(f32[4096]{0:T(1024)} %param.26) | copy-start | bytes 49156
  432.2 3.2 copy-start.1
  441.9 191.8 %reduce-scatter.2.cloned.1.call-start = ((), (), s32[]{:S(2)}) async-start(), calls=%async_computation.4 | async-start | bytes 20480 | tf_op jit(solution)/shard_map/reduce_scatter | solution.py:186
  568.4 47.4 %copy-start.5 = (bf16[512,512]{1,0:T(8,128)(2,1)S(1)}, bf16[512,512]{1,0:T(8,128)(2,1)}, u32[]{:S(2)}) copy-start(bf16[512,512]{1,0:T(8,128)(2,1)} %param.32) | copy-start | bytes 1572868
Sparse Core Ops, SparseCore 0:
  10.2 178.8 all-gather.6
  191.1 72.8 all-gather.8
  273.0 151.3 all-reduce.2
  442.0 125.0 all-gather.10
  616.8 16.7 reduce-scatter.1
where the time goes:
time: 642 us; the launch traced here: 641 us
  waiting for transfers between devices  320 us (50%)
  blocking collectives  188 us (29%)
  matrix products  52.2 us (8%)
  local copies, waits for them, and re-layouts  34.7 us (5%)
  other arithmetic  32.4 us (5%)
  between operations  14.1 us (2%)
    all_gather x1, waiting for transfers between devices, shards(): lax.all_gather(enc_qkv, 'psg', axis=1, tiled=True)  159 us
    all_gather x2, blocking collectives, merged(): everything = jax.tree.map(lambda part: lax.all_gather(part, axis), value)  63.2 us
    all_gather x1, waiting for transfers between devices, merged(): everything = jax.tree.map(lambda part: lax.all_gather(part, axis), value)  61.5 us
    psum x1, waiting for transfers between devices, shards(): summed = lax.psum(partial_out, 'mp').astype(jnp.float32)  53.5 us
    psum x1, blocking collectives, shards(): cross_attn = lax.psum(value_terms, 'psg')  34.2 us
    psum x1, blocking collectives, shards(): cquery = lax.psum(jnp.dot(dquery, query_weight, precision=HIGHEST), 'psg')  33.1 us
    all_gather x1, blocking collectives, shards(): lax.all_gather(folded.astype(jnp.bfloat16), 'psg', axis=2, tiled=True)  31.5 us
    all_gather x1, waiting for transfers between devices, shards(): lax.all_gather(enc_output, 'psg', axis=1, tiled=True)  30.4 us
  transfers between devices with their start and end apart: 5, of which 5 were waited for; matrix products, arithmetic and copies ran while one was open for 12% of the time, Pallas kernels for 0%

commit v1 on v0

--- a/solution.py
+++ b/solution.py
@@ -177,7 +177,11 @@
     )
     value_weight = cross_keyval[1].astype(jnp.float32).reshape(width_here, heads_here, HEAD_DIM)
     value_terms = jnp.einsum("rhd,dhj->rhj", own_pool, value_weight, precision=HIGHEST)
-    cross_attn = lax.psum(value_terms, "psg")
+    cross_attn = value_terms
+    for hop in (1, 2, 4):
+        cross_attn = cross_attn + lax.ppermute(
+            cross_attn, "psg", [(dev, dev ^ hop) for dev in range(8)]
+        )
     out_part = jnp.dot(
         cross_attn.reshape(query_rows, inner_here),
         cross_output.astype(jnp.float32),

time: 642 us -> 622 us (0.969)
  blocking collectives: 188 us -> 154 us
  waiting for transfers between devices: 320 us -> 331 us
    psum x1 -> x0, blocking collectives: 34.2 us -> none  [shards(): cross_attn = lax.psum(value_terms, 'psg')]
    ppermute x0 -> x3, waiting for transfers between devices: none -> 10.6 us  [shards(): lax.ppermute(cross_attn, 'psg', [(dev, dev ^ hop) for dev in range(8)])]
  transfers between devices with their start and end apart: 5 -> 8, of which waited for: 5 -> 8; matrix products, arithmetic and copies ran while one was open for 12% -> 12% of each run, Pallas kernels for 0% -> 0%
where the time goes in v1:
time: 622 us; the launch traced here: 621 us
  waiting for transfers between devices  331 us (53%)
  blocking collectives  154 us (25%)
  matrix products  52.3 us (8%)
  local copies, waits for them, and re-layouts  34.6 us (6%)
  other arithmetic  32.4 us (5%)
  between operations  14 us (2%)
    all_gather x1, waiting for transfers between devices, shards(): lax.all_gather(enc_qkv, 'psg', axis=1, tiled=True)  159 us
    all_gather x2, blocking collectives, merged(): everything = jax.tree.map(lambda part: lax.all_gather(part, axis), value)  63.1 us
    all_gather x1, waiting for transfers between devices, merged(): everything = jax.tree.map(lambda part: lax.all_gather(part, axis), value)  61.6 us
    psum x1, waiting for transfers between devices, shards(): summed = lax.psum(partial_out, 'mp').astype(jnp.float32)  53.5 us
    psum x1, blocking collectives, shards(): cquery = lax.psum(jnp.dot(dquery, query_weight, precision=HIGHEST), 'psg')  33.1 us
    all_gather x1, blocking collectives, shards(): lax.all_gather(folded.astype(jnp.bfloat16), 'psg', axis=2, tiled=True)  31.5 us
    all_gather x1, waiting for transfers between devices, shards(): lax.all_gather(enc_output, 'psg', axis=1, tiled=True)  30.4 us
    psum x1, blocking collectives, shards(): squares_dec = lax.psum(jnp.sum(embedded * embedded, axis=1), 'psg')  19.2 us
  transfers between devices with their start and end apart: 8, of which 8 were waited for; matrix products, arithmetic and copies ran while one was open for 12% of the time, Pallas kernels for 0%

profile of v1, /device:TPU:0, one launch (start us, length us, event | category | flops | bytes accessed | tf_op | source)
XLA Modules:
  0.0 620.8 jit_solution(15320351865871725227)
XLA Ops:
  10.4 2.2 slice.61
  12.7 7.9 %reshape.172 = f32[8,256,511]{2,1,0:T(8,128)} reshape(f32[8,130816]{1,0:T(8,128)} %slice.61) | data formatting | bytes 8372224 | tf_op jit(solution)/shard_map/reshape | solution.py:61
  20.5 2.2 slice.62
  24.9 5.1 fusion.7
  29.9 159.1 %all-gather.7.cloned.1.call-done = bf16[3,4096,512]{2,1,0:T(8,128)(2,1)} async-done(((bf16[3,512,512]{2,1,0:T(8,128)(2,1)}), bf16[3,4096,512]{2,1,0:T(8,128)(2,1)}) %all-gather.7.cloned.1.call-update) | async-done | bytes 12582928 | tf_op jit(solution)/shard_map/all_gather | solution.py:111
  189.0 18.3 %convert_bitcast_fusion = bf16[3,1024,512]{2,1,0:T(8,128)(2,1)S(1)} fusion(bf16[3,4096,512]{2,1,0:T(8,128)(2,1)} %all-gather.7.cloned.1.call-done, bf16[1024,4096]{1,0:T(8,128)(2,1)} %param.18, f32[4096]{0:T(1024)S(1)} %copy-done.10, f32[1024]{0:T(1024)S(1)} %add_rsqrt_fusion.1), kind=kOutput, calls=%fused_computation.37 | convolution fusion | flops 12903251968 | bytes 24137728 | tf_op jit(solution)/shard_map/td,kdc->ktc/dot_general | solution.py:108
  209.1 2.8 reshape.191
  211.9 3.9 reshape.192
  215.7 3.9 reshape.190
  219.6 3.0 fusion.28
  222.6 5.4 fusion.64
  228.0 4.5 fusion.35
  233.5 30.4 %all-gather.9.cloned.1.call-done = bf16[512,4096]{1,0:T(8,128)(2,1)} async-done(((bf16[512,512]{1,0:T(8,128)(2,1)}), bf16[512,4096]{1,0:T(8,128)(2,1)}) %all-gather.9.cloned.1.call-update) | async-done | bytes 4194320 | tf_op jit(solution)/shard_map/all_gather | solution.py:135
  263.9 8.9 %convolution_convert_fusion = bf16[1024,4096]{1,0:T(8,128)(2,1)} fusion(bf16[1024,512]{0,1:T(8,128)(2,1)S(1)} %bitcast.81, bf16[512,4096]{1,0:T(8,128)(2,1)} %all-gather.9.cloned.1.call-done), kind=kOutput, calls=%fused_computation.29 | convolution fusion | flops 4299161600 | bytes 13631488 | tf_op jit(solution)/shard_map/dot_general | solution.py:133
  273.7 5.1 convolution_convert_fusion.2
  278.8 6.7 %psum.29 = bf16[8,512]{1,0:T(8,128)(2,1)S(1)} all-reduce(bf16[8,512]{1,0:T(8,128)(2,1)S(1)} %convolution_convert_fusion.2), channel_id=1, replica_groups=mesh['psg'=8,'mp'=4] {'mp'}, use_global_device_ids=true, to_apply=%region_4.5 | all-reduce | flops 4096 | bytes 16384 | tf_op jit(solution)/shard_map/psum | solution.py:146
  285.7 19.2 %psum.30 = f32[8]{0:T(128)S(1)} all-reduce(f32[8]{0:T(128)S(1)} %multiply_reduce_fusion), channel_id=1, replica_groups=mesh['psg'=8,'mp'=4] {'psg'}, use_global_device_ids=true, to_apply=%region_6.7 | all-reduce | flops 8 | bytes 64 | tf_op jit(solution)/shard_map/psum | solution.py:148
  305.8 33.1 %psum.31 = f32[8,8,64]{2,0,1:T(8,128)S(1)} all-reduce(f32[8,8,64]{2,0,1:T(8,128)S(1)} %copy.49), channel_id=1, replica_groups=mesh['psg'=8,'mp'=4] {'psg'}, use_global_device_ids=true, to_apply=%region_7.8 | all-reduce | flops 4096 | bytes 32768 | tf_op jit(solution)/shard_map/psum | solution.py:150
  339.4 31.5 %all_gather.29 = bf16[8,8,4096]{2,0,1:T(8,128)(2,1)S(1)} all-gather(bf16[8,8,512]{2,0,1:T(8,128)(2,1)S(1)} %fusion.44), channel_id=1, replica_groups=mesh['psg'=8,'mp'=4] {'psg'}, dimensions={2}, use_global_device_ids=true | all-gather | bytes 589824 | tf_op jit(solution)/shard_map/all_gather | solution.py:160
  370.9 53.5 %all-reduce.3.cloned.1.call-done = bf16[1024,4096]{1,0:T(8,128)(2,1)} async-done(((bf16[1024,4096]{1,0:T(8,128)(2,1)}), bf16[1024,4096]{1,0:T(8,128)(2,1)}) %all-reduce.3.cloned.1.call-update) | async-done | bytes 8388624 | tf_op jit(solution)/shard_map/psum | solution.py:138
  424.4 7.8 %fusion.4 = (f32[1024]{0:T(1024)S(1)}, bf16[1024,4096]{1,0:T(8,128)(2,1)S(1)}) fusion(bf16[1024,4096]{1,0:T(8,128)(2,1)} %all-reduce.3.cloned.1.call-done, bf16[1024,4096]{1,0:T(8,128)(2,1)} %param.18), kind=kLoop, calls=%fused_computation.14 | loop fusion | flops 29359104 | bytes 25169920 | tf_op jit(solution)/shard_map/reduce_sum | solution.py:66
  432.2 2.9 fusion.65
  435.4 6.4 %fusion.18 = f32[8,8,4096]{2,1,0:T(8,128)} fusion(bf16[1024,4096]{1,0:T(8,128)(2,1)S(1)} %get-tuple-element.200, f32[4096]{0:T(1024)S(1)} %copy-done.11, f32[1024]{0:T(1024)S(1)} %add_rsqrt_fusion, f32[8,8,1024]{2,1,0:T(8,128)S(1)} %get-tuple-element.209, f32[8,8]{1,0:T(8,128)S(1)} %get-tuple-element.208, pred[8,1024]{1,0:T(8,128)(4,1)S(1)} %broadcast_and_fusion), kind=kOutput, calls=%fused_computation.31 | convolution fusion | flops 3238133760 | bytes 9728256 | tf_op jit(solution)/shard_map/rht,td->rhd/dot_general | solution.py:170
  442.3 31.6 %all-gather.1 = f32[64,8]{1,0:T(8,128)S(1)} all-gather(f32[8,8]{1,0:T(8,128)S(1)} %fusion.46), channel_id=3, replica_groups=mesh['psg'=8,'mp'=4] {'psg'}, dimensions={0}, use_global_device_ids=true | all-gather | bytes 2304 | tf_op jit(solution)/shard_map/all_gather | solution.py:21
  473.9 31.5 %all-gather = f32[64,8]{1,0:T(8,128)S(1)} all-gather(f32[8,8]{1,0:T(8,128)S(1)} %get-tuple-element.208), channel_id=2, replica_groups=mesh['psg'=8,'mp'=4] {'psg'}, dimensions={0}, use_global_device_ids=true | all-gather | bytes 2304 | tf_op jit(solution)/shard_map/all_gather | solution.py:21
  505.5 61.6 %all-gather.11.cloned.1.call-done = f32[64,8,4096]{2,1,0:T(8,128)} async-done(((f32[8,8,4096]{2,1,0:T(8,128)}), f32[64,8,4096]{2,1,0:T(8,128)}) %all-gather.11.cloned.1.call-update) | async-done | bytes 8388624 | tf_op jit(solution)/shard_map/all_gather | solution.py:21
  568.4 12.4 %while.19 = (s32[]{:T(128)}, f32[8,8]{1,0:T(8,128)S(1)}, f32[8,8]{1,0:T(8,128)S(1)}, f32[8,8,4096]{2,1,0:T(8,128)S(1)}, f32[8,8,8]{2,1,0:T(8,128)S(1)}, /*index=...) while((s32[]{:T(128)}, f32[8,8]{1,0:T(8,128)S(1)}, ...), condition=%wide.region_12.13_spmd, body=%wide.region_11.12_spmd.sunk | while | flops 786821 | bytes 3148439 | solution.py:27
  582.0 3.4 collective-permute-done
  585.4 3.9 collective-permute-done.1
  590.8 3.3 collective-permute-done.2
  595.2 3.1 constant_dynamic-slice_fusion
  598.2 14.8 %reduce-scatter.2.cloned.1.call-done = f32[8,128]{1,0:T(8,128)} async-done(((f32[8,512]{1,0:T(8,128)}), f32[8,128]{1,0:T(8,128)}) %reduce-scatter.2.cloned.1.call-update) | async-done | bytes 4112 | tf_op jit(solution)/shard_map/reduce_scatter | solution.py:190
  (101 shorter events, 29.6 us)
Async XLA Ops:
  7.2 297.7 %copy-start = (bf16[512,512]{1,0:T(8,128)(2,1)S(1)}, bf16[512,512]{1,0:T(8,128)(2,1)}, u32[]{:S(2)}) copy-start(bf16[512,512]{1,0:T(8,128)(2,1)} %param.30) | copy-start | bytes 1572868
  7.2 181.8 %all-gather.7.cloned.1.call-start = ((), (), s32[]{:S(2)}) async-start(), calls=%async_computation.1 | async-start | bytes 14155776 | tf_op jit(solution)/shard_map/all_gather | solution.py:111
  7.9 256.0 %all-gather.9.cloned.1.call-start = ((), (), s32[]{:S(2)}) async-start(), calls=%async_computation.2 | async-start | bytes 4718592 | tf_op jit(solution)/shard_map/all_gather | solution.py:135
  8.7 415.7 %all-reduce.3.cloned.1.call-start = ((), (), s32[]{:S(2)}) async-start(), calls=%async_computation.3 | async-start | bytes 16777216 | tf_op jit(solution)/shard_map/psum | solution.py:138
  12.6 12.1 %copy-start.9 = (s32[4]{0:T(128)S(1)}, s32[4]{0:T(128)}, u32[]{:S(2)}) copy-start(s32[4]{0:T(128)} %param.19) | copy-start | bytes 52
  20.5 168.5 %copy-start.10 = (f32[4096]{0:T(1024)S(1)}, f32[4096]{0:T(1024)}, u32[]{:S(2)}) copy-start(f32[4096]{0:T(1024)} %param.22) | copy-start | bytes 49156
  219.6 3.0 copy-start.3
  222.6 5.4 copy-start.2
  272.9 0.7 copy-start.7
  272.9 32.0 %copy-start.6 = (f32[512]{0:T(512)S(1)}, f32[512]{0:T(512)}, u32[]{:S(2)}) copy-start(f32[512]{0:T(512)} %param.29) | copy-start | bytes 6148
  272.9 32.4 %copy-start.4 = (bf16[2,512,512]{2,1,0:T(8,128)(2,1)S(1)}, bf16[2,512,512]{2,1,0:T(8,128)(2,1)}, u32[]{:S(2)}) copy-start(bf16[2,512,512]{2,1,0:T(8,128)(2,1)} %param.31) | copy-start | bytes 3145732
  272.9 294.2 %all-gather.11.cloned.1.call-start = ((), (), s32[]{:S(2)}) async-start(), calls=%async_computation.5 | async-start | bytes 9437184 | tf_op jit(solution)/shard_map/all_gather | solution.py:21
  273.7 31.9 %copy-start.8 = (f32[4]{0:T(128)S(1)}, f32[4]{0:T(128)}, u32[]{:S(2)}) copy-start(f32[4]{0:T(128)} %param.21) | copy-start | bytes 52
  273.7 65.2 %copy-start.12 = (s32[4]{0:T(128)S(1)}, s32[4]{0:T(128)}, u32[]{:S(2)}) copy-start(s32[4]{0:T(128)} %param.20) | copy-start | bytes 52
  370.9 61.3 %copy-start.11 = (f32[4096]{0:T(1024)S(1)}, f32[4096]{0:T(1024)}, u32[]{:S(2)}) copy-start(f32[4096]{0:T(1024)} %param.26) | copy-start | bytes 49156
  432.2 3.2 copy-start.1
  441.9 171.2 %reduce-scatter.2.cloned.1.call-start = ((), (), s32[]{:S(2)}) async-start(), calls=%async_computation.4 | async-start | bytes 20480 | tf_op jit(solution)/shard_map/reduce_scatter | solution.py:190
  568.4 25.8 %copy-start.5 = (bf16[512,512]{1,0:T(8,128)(2,1)S(1)}, bf16[512,512]{1,0:T(8,128)(2,1)}, u32[]{:S(2)}) copy-start(bf16[512,512]{1,0:T(8,128)(2,1)} %param.32) | copy-start | bytes 1572868
  581.4 3.9 collective-permute-start
  585.4 3.9 collective-permute-start.1
  589.3 4.8 collective-permute-start.2
Sparse Core Ops, SparseCore 0:
  10.2 178.8 all-gather.6
  191.1 72.8 all-gather.8
  273.0 151.3 all-reduce.2
  442.0 125.0 all-gather.10
  595.3 17.7 reduce-scatter.1
